TPU v7x, 32 devices: a whole 2x2x4 slice. The times are simulated.
32 devices in a mesh: frame: 4 (over y, x), vox: 8 (over z, core).
Axes of the slice: x: 2, y: 2, z: 4, core: 2. Of those that a mesh axis runs over, the one named last changes fastest.
Arguments:
- pool: bfloat16 [2048, 8192], P('frame', 'vox'), may hold values from -6 to 6
- dictionary: bfloat16 [1024, 8192], P(None, 'vox'), may hold values from -0.13258252 to 0.13258252
- support: int32 [1024, 64], P(None, 'vox'), may hold values from 0 to 1, as said below
- pick: int32 [1024], P('frame'), may hold values from 0 to 511
Outputs:
- codes: bfloat16 [1024, 1024], P('frame')
- gradient: float32 [1024, 8192], P('frame', 'vox')
Inputs may be any that keep to these rules, and one draw needn't show every extreme that they name: Every mode has at least one voxel block in its support.
All inputs are finite; a program needn't handle non-finite values.
Results may differ from a plain program's by a relative error of at most 0.015.
Values may be sent and summed in bfloat16 or wider, within the bound.
No kernel may reach another device: no remote copies, remote signals or barrier semaphores. Data moves between devices by JAX's collectives and lax.ppermute only.
A program may use at most 64 MiB of HBM per device.

v0:
```python
import jax
import jax.numpy as jnp
from jax import lax
from jax.sharding import PartitionSpec as P

BLOCK = 128


def shrink(value, limit):
    return jnp.sign(value) * jnp.maximum(jnp.abs(value) - limit, 0.0)


def against(left, right):
    return lax.dot_general(
        left, right, (((1,), (1,)), ((), ())), preferred_element_type=jnp.float32
    )


def body(pool, dictionary, support, pick):
    batch = pool[pick]
    batch_wide = batch.astype(jnp.float32)
    keep = jnp.repeat(support, BLOCK, axis=1).astype(jnp.bfloat16)
    masked = dictionary * keep
    corr_local = against(batch, masked)
    energy_local = jnp.sum(jnp.square(masked.astype(jnp.float32)), axis=1)
    corr, energy = lax.psum((corr_local, energy_local), "vox")
    step = 1.0 / (energy + 1e-05)
    first = shrink(corr * step, 0.3 * step).astype(jnp.bfloat16)
    resid = (jnp.dot(first, masked, preferred_element_type=jnp.float32) - batch_wide).astype(
        jnp.bfloat16
    )
    push = lax.psum(against(resid, masked), "vox")
    codes = shrink(first.astype(jnp.float32) - step * push, 0.3 * step).astype(jnp.bfloat16)
    error = (jnp.dot(codes, masked, preferred_element_type=jnp.float32) - batch_wide).astype(
        jnp.bfloat16
    )
    groups = lax.axis_size("frame")
    own_rows = support.shape[0] // groups
    summed = lax.psum_scatter(
        lax.dot_general(
            codes, error, (((0,), (0,)), ((), ())), preferred_element_type=jnp.float32
        ).astype(jnp.bfloat16),
        "frame",
        scatter_dimension=0,
        tiled=True,
    ).astype(jnp.float32)
    keep_rows = lax.dynamic_slice_in_dim(keep, lax.axis_index("frame") * own_rows, own_rows, 0)
    gradient = keep_rows.astype(jnp.float32) * summed / (batch.shape[0] * groups)
    return (codes, gradient)


def solution(mesh):
    placed = (P("frame", "vox"), P(None, "vox"), P(None, "vox"), P("frame"))
    return jax.shard_map(
        body,
        mesh=mesh,
        in_specs=placed,
        out_specs=(P("frame", None), P("frame", "vox")),
        check_vma=False,
    )
```

profile of v0, /device:TPU:0, one launch (start us, length us, event | category | flops | bytes accessed | tf_op | source)
XLA Modules:
  0.0 196.3 jit_solution(7475399886197143005)
XLA Ops:
  7.2 0.0 copy-start
  7.2 0.0 all-reduce.3.cloned.1.call-start
  7.2 0.8 convert_element_type.37
  8.1 0.2 copy.6
  8.2 0.0 copy-start.1
  8.3 0.8 compare_select_fusion
  9.1 2.9 %broadcast_in_dim.5 = bf16[1024,8,128]{2,1,0:T(8,128)(2,1)S(1)} broadcast(bf16[1024,8]{1,0:T(8,128)(2,1)S(1)} %copy.6), dimensions={0,1} | broadcast | bytes 2113536 | tf_op jit(solution)/shard_map/broadcast_in_dim | solution.py:22
  12.0 0.0 copy-done.1
  12.0 2.1 %multiply_reduce_fusion = (f32[1024]{0:T(1024)S(1)}, bf16[1024,1024]{1,0:T(8,128)(2,1)}) fusion(bf16[1024,1024]{1,0:T(8,128)(2,1)S(1)} %copy-done.1, bf16[128,8,8,128]{3,2,1,0:T(8,128)(2,1)S(1)} %bitcast.14), kind=kLoop, calls=%fused_computation.1 | loop fusion | flops 4193280 | bytes 6295552 | tf_op jit(solution)/shard_map/reduce_sum | solution.py:25
  14.1 0.0 copy-done
  14.1 2.0 gather_fusion
  16.1 3.5 %fusion.5 = f32[256,1024]{1,0:T(8,128)} fusion(bf16[256,1024]{1,0:T(8,128)(2,1)} %gather_fusion, bf16[1024,1024]{1,0:T(8,128)(2,1)} %get-tuple-element.3), kind=kOutput, calls=%fused_computation.17 | convolution fusion | flops 536870912 | bytes 3670016 | tf_op jit(solution)/shard_map/dot_general | solution.py:14
  19.6 0.0 all-reduce.3.cloned.1.call-update
  19.6 0.0 all-reduce.5.cloned.1.call-start
  19.6 18.4 %psum.22 = f32[1024]{0:T(1024)S(1)} all-reduce(f32[1024]{0:T(1024)S(1)} %get-tuple-element.2), channel_id=1, replica_groups=mesh['frame'=4,'vox'=8] {'vox'}, use_global_device_ids=true, to_apply=%region_2.0 | all-reduce | flops 1024 | bytes 8192 | tf_op jit(solution)/shard_map/psum | solution.py:26
  38.1 43.5 %all-reduce.3.cloned.1.call-done = f32[256,1024]{1,0:T(8,128)} async-done(((f32[256,1024]{1,0:T(8,128)}), f32[256,1024]{1,0:T(8,128)}) %all-reduce.3.cloned.1.call-update) | async-done | bytes 1048592 | tf_op jit(solution)/shard_map/psum | solution.py:26
  81.6 5.1 %fusion.2 = f32[256,1024]{1,0:T(8,128)} fusion(bf16[1024,1024]{1,0:T(8,128)(2,1)} %get-tuple-element.3, bf16[256,1024]{1,0:T(8,128)(2,1)} %gather_fusion, f32[256,1024]{1,0:T(8,128)} %all-reduce.3.cloned.1.call-done, f32[1024]{0:T(1024)S(1)} %get-tuple-element.5, f32[1024]{0:T(1024)S(1)} %get-tuple-element.4), kind=kOutput, calls=%fused_computation.11 | convolution fusion | flops 1076363264 | bytes 4726784 | tf_op jit(solution)/shard_map/dot_general | solution.py:14
  86.7 0.0 all-reduce.5.cloned.1.call-update
  86.7 0.0 reduce-scatter.2.cloned.1.call-start
  86.8 58.4 %all-reduce.5.cloned.1.call-done = f32[256,1024]{1,0:T(8,128)} async-done(((f32[256,1024]{1,0:T(8,128)}), f32[256,1024]{1,0:T(8,128)}) %all-reduce.5.cloned.1.call-update) | async-done | bytes 1048592 | tf_op jit(solution)/shard_map/psum | solution.py:32
  145.2 3.2 %multiply_convert_fusion = bf16[256,1024]{1,0:T(8,128)(2,1)} fusion(f32[256,1024]{1,0:T(8,128)} %all-reduce.5.cloned.1.call-done, f32[1024]{0:T(1024)S(1)} %get-tuple-element.5, f32[1024]{0:T(1024)S(1)} %get-tuple-element.4, f32[256,1024]{1,0:T(8,128)} %all-reduce.3.cloned.1.call-done), kind=kLoop, calls=%fused_computation.9 | loop fusion | flops 4194304 | bytes 2629632 | tf_op jit(solution)/shard_map/convert_element_type | solution.py:33
  148.4 4.5 %convolution_convert_fusion = bf16[1024,1024]{1,0:T(8,128)(2,1)} fusion(bf16[256,1024]{1,0:T(8,128)(2,1)} %multiply_convert_fusion, bf16[256,1024]{1,0:T(8,128)(2,1)} %gather_fusion, bf16[1024,1024]{1,0:T(8,128)(2,1)} %get-tuple-element.3), kind=kOutput, calls=%fused_computation.3 | convolution fusion | flops 1075576832 | bytes 5242880 | tf_op jit(solution)/shard_map/dot_general | solution.py:40
  152.9 0.0 reduce-scatter.2.cloned.1.call-update
  153.0 2.0 %copy.12 = bf16[128,8,8,128]{3,1,2,0:T(8,128)(2,1)} copy(bf16[128,8,8,128]{3,2,1,0:T(8,128)(2,1)S(1)} %bitcast.15) | data formatting | bytes 4194304
  155.0 32.4 %reduce-scatter.2.cloned.1.call-done = bf16[256,1024]{1,0:T(8,128)(2,1)} async-done(((bf16[1024,1024]{1,0:T(8,128)(2,1)}), bf16[256,1024]{1,0:T(8,128)(2,1)}) %reduce-scatter.2.cloned.1.call-update) | async-done | bytes 524304 | tf_op jit(solution)/shard_map/reduce_scatter | solution.py:39
  187.4 2.4 %multiply_multiply_fusion = f32[256,1024]{1,0:T(8,128)} fusion(bf16[256,1024]{1,0:T(8,128)(2,1)} %reduce-scatter.2.cloned.1.call-done, bf16[1024,1024]{1,0:T(8,128)(2,1)} %bitcast.16, s32[]{:T(128)S(6)} %select_n.7), kind=kLoop, calls=%fused_computation.8 | loop fusion | flops 1048576 | bytes 2097156 | tf_op jit(solution)/shard_map/div | solution.py:48
  (2 shorter events, 0.0 us)
Async XLA Ops:
  7.2 7.0 %copy-start = (bf16[512,1024]{1,0:T(8,128)(2,1)S(1)}, bf16[512,1024]{1,0:T(8,128)(2,1)}, u32[]{:S(2)}) copy-start(bf16[512,1024]{1,0:T(8,128)(2,1)} %param.4) | copy-start | bytes 3145732
  7.2 74.4 %all-reduce.3.cloned.1.call-start = ((), (), s32[]{:S(2)}) async-start(), calls=%async_computation.1 | async-start | bytes 2097152 | tf_op jit(solution)/shard_map/psum | solution.py:26
  8.2 3.8 %copy-start.1 = (bf16[1024,1024]{1,0:T(8,128)(2,1)S(1)}, bf16[1024,1024]{1,0:T(8,128)(2,1)}, u32[]{:S(2)}) copy-start(bf16[1024,1024]{1,0:T(8,128)(2,1)} %param.5) | copy-start | bytes 6291460
  19.6 125.6 %all-reduce.5.cloned.1.call-start = ((), (), s32[]{:S(2)}) async-start(), calls=%async_computation.2 | async-start | bytes 2097152 | tf_op jit(solution)/shard_map/psum | solution.py:32
  86.7 100.6 %reduce-scatter.2.cloned.1.call-start = ((), (), s32[]{:S(2)}) async-start(), calls=%async_computation.3 | async-start | bytes 2621440 | tf_op jit(solution)/shard_map/reduce_scatter | solution.py:39
Sparse Core Ops, SparseCore 0:
  19.7 61.8 all-reduce.2
  86.9 58.2 all-reduce.4
  153.1 34.2 reduce-scatter.1
where the time goes:
time: 197 us; the launch traced here: 196 us
  waiting for transfers between devices  134 us (68%)
  blocking collectives  18.4 us (9%)
  between operations  13.8 us (7%)
  matrix products  13.1 us (7%)
  other arithmetic  9.34 us (5%)
  local copies, waits for them, and re-layouts  7.04 us (4%)
    psum x1, waiting for transfers between devices, body(): push = lax.psum(against(resid, masked), 'vox')  58.4 us
    psum x1, waiting for transfers between devices, body(): corr, energy = lax.psum((corr_local, energy_local), 'vox')  43.5 us
    reduce_scatter x1, waiting for transfers between devices, body(): lax.psum_scatter(lax.dot_general(codes, error, (((0,), (0,)), ((), ())),...  32.4 us
    psum x1, blocking collectives, body(): corr, energy = lax.psum((corr_local, energy_local), 'vox')  18.4 us
    dot_general x2, matrix products, against(): lax.dot_general(left, right, (((1,), (1,)), ((), ())), preferred_element_...  8.6 us
    dot_general x1, matrix products, body(): lax.dot_general(codes, error, (((0,), (0,)), ((), ())), preferred_element...  4.54 us
  transfers between devices with their start and end apart: 3, of which 3 were waited for; matrix products, arithmetic and copies ran while one was open for 1% of the time, Pallas kernels for 0%

commit v1 on v0

--- a/solution.py
+++ b/solution.py
@@ -29,7 +29,7 @@
     resid = (jnp.dot(first, masked, preferred_element_type=jnp.float32) - batch_wide).astype(
         jnp.bfloat16
     )
-    push = lax.psum(against(resid, masked), "vox")
+    push = jnp.sum(lax.all_gather(against(resid, masked), "vox"), axis=0)
     codes = shrink(first.astype(jnp.float32) - step * push, 0.3 * step).astype(jnp.bfloat16)
     error = (jnp.dot(codes, masked, preferred_element_type=jnp.float32) - batch_wide).astype(
         jnp.bfloat16

time: 197 us -> 224 us (1.14)
  waiting for transfers between devices: 134 us -> 157 us
  other arithmetic: 9.34 us -> 14.7 us
    all_gather x0 -> x1, waiting for transfers between devices: none -> 81.2 us  [body(): push = jnp.sum(lax.all_gather(against(resid, masked), 'vox'), axis=0)]
    psum x1 -> x0, waiting for transfers between devices: 58.4 us -> none  [body(): push = lax.psum(against(resid, masked), 'vox')]
    reduce_sum x0 -> x1, other arithmetic: none -> 5.35 us  [body(): push = jnp.sum(lax.all_gather(against(resid, masked), 'vox'), axis=0)]
where the time goes in v1:
time: 224 us
  waiting for transfers between devices  157 us (70%)
  blocking collectives  18.4 us (8%)
  other arithmetic  14.7 us (7%)
  between operations  13.8 us (6%)
  matrix products  13.3 us (6%)
  local copies, waits for them, and re-layouts  6.99 us (3%)
    all_gather x1, waiting for transfers between devices, body(): push = jnp.sum(lax.all_gather(against(resid, masked), 'vox'), axis=0)  81.2 us
    psum x1, waiting for transfers between devices, body(): corr, energy = lax.psum((corr_local, energy_local), 'vox')  43.5 us
    reduce_scatter x1, waiting for transfers between devices, body(): lax.psum_scatter(lax.dot_general(codes, error, (((0,), (0,)), ((), ())),...  31.9 us
    psum x1, blocking collectives, body(): corr, energy = lax.psum((corr_local, energy_local), 'vox')  18.4 us
    dot_general x2, matrix products, against(): lax.dot_general(left, right, (((1,), (1,)), ((), ())), preferred_element_...  8.66 us
    reduce_sum x1, other arithmetic, body(): push = jnp.sum(lax.all_gather(against(resid, masked), 'vox'), axis=0)  5.35 us
    dot_general x1, matrix products, body(): lax.dot_general(codes, error, (((0,), (0,)), ((), ())), preferred_element...  4.6 us
  transfers between devices with their start and end apart: 3, of which 3 were waited for; matrix products, arithmetic and copies ran while one was open for 1% of the time, Pallas kernels for 0%

profile of v1, /device:TPU:0, one launch (start us, length us, event | category | flops | bytes accessed | tf_op | source)
XLA Modules:
  0.0 224.0 jit_solution(7031434229714498948)
XLA Ops:
  7.2 0.0 copy-start
  7.2 0.0 all-reduce.2.cloned.1.call-start
  7.2 0.8 convert_element_type.37
  8.1 0.2 copy.6
  8.2 0.0 copy-start.1
  8.3 0.8 compare_select_fusion
  9.1 2.9 %broadcast_in_dim.5 = bf16[1024,8,128]{2,1,0:T(8,128)(2,1)S(1)} broadcast(bf16[1024,8]{1,0:T(8,128)(2,1)S(1)} %copy.6), dimensions={0,1} | broadcast | bytes 2113536 | tf_op jit(solution)/shard_map/broadcast_in_dim | solution.py:22
  12.0 0.0 copy-done.1
  12.0 2.1 multiply_reduce_fusion
  14.2 0.0 copy-done
  14.2 2.0 gather_fusion
  16.1 3.5 %fusion.5 = f32[256,1024]{1,0:T(8,128)} fusion(bf16[256,1024]{1,0:T(8,128)(2,1)} %gather_fusion, bf16[1024,1024]{1,0:T(8,128)(2,1)} %get-tuple-element.3), kind=kOutput, calls=%fused_computation.17 | convolution fusion | flops 536870912 | bytes 3670016 | tf_op jit(solution)/shard_map/dot_general | solution.py:14
  19.6 0.0 all-reduce.2.cloned.1.call-update
  19.6 0.0 all-gather.3.cloned.1.call-start
  19.7 18.4 %psum.15 = f32[1024]{0:T(1024)S(1)} all-reduce(f32[1024]{0:T(1024)S(1)} %get-tuple-element.2), channel_id=1, replica_groups=mesh['frame'=4,'vox'=8] {'vox'}, use_global_device_ids=true, to_apply=%region_2.0 | all-reduce | flops 1024 | bytes 8192 | tf_op jit(solution)/shard_map/psum | solution.py:26
  38.1 43.5 %all-reduce.2.cloned.1.call-done = f32[256,1024]{1,0:T(8,128)} async-done(((f32[256,1024]{1,0:T(8,128)}), f32[256,1024]{1,0:T(8,128)}) %all-reduce.2.cloned.1.call-update) | async-done | bytes 1048592 | tf_op jit(solution)/shard_map/psum | solution.py:26
  81.6 5.2 %fusion.2 = f32[256,1024]{1,0:T(8,128)} fusion(bf16[1024,1024]{1,0:T(8,128)(2,1)} %get-tuple-element.3, bf16[256,1024]{1,0:T(8,128)(2,1)} %gather_fusion, f32[256,1024]{1,0:T(8,128)} %all-reduce.2.cloned.1.call-done, f32[1024]{0:T(1024)S(1)} %get-tuple-element.5, f32[1024]{0:T(1024)S(1)} %get-tuple-element.4), kind=kOutput, calls=%fused_computation.11 | convolution fusion | flops 1076363264 | bytes 4726784 | tf_op jit(solution)/shard_map/dot_general | solution.py:14
  86.8 0.0 all-gather.3.cloned.1.call-update
  86.8 0.0 reduce-scatter.2.cloned.1.call-start
  86.9 81.2 %all-gather.3.cloned.1.call-done = f32[2048,1024]{1,0:T(8,128)} async-done(((f32[256,1024]{1,0:T(8,128)}), f32[2048,1024]{1,0:T(8,128)}) %all-gather.3.cloned.1.call-update) | async-done | bytes 8388624 | tf_op jit(solution)/shard_map/all_gather | solution.py:32
  168.1 5.3 %reduce_sum.19 = f32[256,1024]{1,0:T(8,128)} reduce(f32[8,256,1024]{2,1,0:T(8,128)} %bitcast.17, f32[]{:T(128)} %constant.3.clone.1), dimensions={0}, to_apply=%region_3.0 | reduce | flops 1835008 | bytes 9437188 | tf_op jit(solution)/shard_map/reduce_sum | solution.py:32
  173.4 3.2 %multiply_convert_fusion = bf16[256,1024]{1,0:T(8,128)(2,1)} fusion(f32[256,1024]{1,0:T(8,128)} %reduce_sum.19, f32[1024]{0:T(1024)S(1)} %get-tuple-element.5, f32[1024]{0:T(1024)S(1)} %get-tuple-element.4, f32[256,1024]{1,0:T(8,128)} %all-reduce.2.cloned.1.call-done), kind=kLoop, calls=%fused_computation.9 | loop fusion | flops 4194304 | bytes 2629632 | tf_op jit(solution)/shard_map/convert_element_type | solution.py:33
  176.6 4.6 %convolution_convert_fusion = bf16[1024,1024]{1,0:T(8,128)(2,1)} fusion(bf16[256,1024]{1,0:T(8,128)(2,1)} %multiply_convert_fusion, bf16[256,1024]{1,0:T(8,128)(2,1)} %gather_fusion, bf16[1024,1024]{1,0:T(8,128)(2,1)} %get-tuple-element.3), kind=kOutput, calls=%fused_computation.3 | convolution fusion | flops 1075576832 | bytes 5242880 | tf_op jit(solution)/shard_map/dot_general | solution.py:40
  181.2 0.0 reduce-scatter.2.cloned.1.call-update
  181.2 1.9 copy.12
  183.2 31.9 %reduce-scatter.2.cloned.1.call-done = bf16[256,1024]{1,0:T(8,128)(2,1)} async-done(((bf16[1024,1024]{1,0:T(8,128)(2,1)}), bf16[256,1024]{1,0:T(8,128)(2,1)}) %reduce-scatter.2.cloned.1.call-update) | async-done | bytes 524304 | tf_op jit(solution)/shard_map/reduce_scatter | solution.py:39
  215.1 2.4 %multiply_multiply_fusion = f32[256,1024]{1,0:T(8,128)} fusion(bf16[256,1024]{1,0:T(8,128)(2,1)} %reduce-scatter.2.cloned.1.call-done, bf16[1024,1024]{1,0:T(8,128)(2,1)} %bitcast.18, s32[]{:T(128)S(6)} %select_n.7), kind=kLoop, calls=%fused_computation.8 | loop fusion | flops 1048576 | bytes 2097156 | tf_op jit(solution)/shard_map/div | solution.py:48
  (2 shorter events, 0.0 us)
Async XLA Ops:
  7.2 7.0 %copy-start = (bf16[512,1024]{1,0:T(8,128)(2,1)S(1)}, bf16[512,1024]{1,0:T(8,128)(2,1)}, u32[]{:S(2)}) copy-start(bf16[512,1024]{1,0:T(8,128)(2,1)} %param.4) | copy-start | bytes 3145732
  7.2 74.4 %all-reduce.2.cloned.1.call-start = ((), (), s32[]{:S(2)}) async-start(), calls=%async_computation.1 | async-start | bytes 2097152 | tf_op jit(solution)/shard_map/psum | solution.py:26
  8.2 3.8 %copy-start.1 = (bf16[1024,1024]{1,0:T(8,128)(2,1)S(1)}, bf16[1024,1024]{1,0:T(8,128)(2,1)}, u32[]{:S(2)}) copy-start(bf16[1024,1024]{1,0:T(8,128)(2,1)} %param.5) | copy-start | bytes 6291460
  19.6 148.4 %all-gather.3.cloned.1.call-start = ((), (), s32[]{:S(2)}) async-start(), calls=%async_computation.3 | async-start | bytes 9437184 | tf_op jit(solution)/shard_map/all_gather | solution.py:32
  86.8 128.3 %reduce-scatter.2.cloned.1.call-start = ((), (), s32[]{:S(2)}) async-start(), calls=%async_computation.2 | async-start | bytes 2621440 | tf_op jit(solution)/shard_map/reduce_scatter | solution.py:39
Sparse Core Ops, SparseCore 0:
  19.8 61.8 all-reduce.1
  86.9 81.0 all-gather.2
  181.4 33.6 reduce-scatter.1
